TPU v7x, 32 devices: a whole 2x2x4 slice. The times are simulated.
32 devices in a mesh: grp: 2 (over y), depth: 4 (over z), shot: 2 (over x), lat: 2 (over core).
Axes of the slice: x: 2, y: 2, z: 4, core: 2. Of those that a mesh axis runs over, the one named last changes fastest.
Arguments:
- fwd_prev: float32 [8, 8, 128, 128], P(('grp', 'shot'), 'depth', 'lat'), parts along dimension 0, may hold values from -6 to 6
- fwd_now: float32 [8, 8, 128, 128], P(('grp', 'shot'), 'depth', 'lat'), parts along dimension 0, may hold values from -6 to 6
- adj_late: float32 [8, 8, 128, 128], P(('grp', 'shot'), 'depth', 'lat'), parts along dimension 0, may hold values from -6 to 6
- adj_last: float32 [8, 8, 128, 128], P(('grp', 'shot'), 'depth', 'lat'), parts along dimension 0, may hold values from -6 to 6
- velocity: float32 [16, 128, 128], P(('grp', 'depth'), 'lat', 'shot'), parts along dimension 0, may hold values from 1.5 to 4.5
- density: float32 [16, 128, 128], P(('grp', 'depth'), 'lat'), parts along dimension 0, may hold values from 1.5 to 2.5
- wavelet: float32 [8, 2], P(('grp', 'shot')), parts along dimension 0, may hold values from -48 to 48
- source_cell: int32 [8], P(('grp', 'shot')), parts along dimension 0, may hold values from 0 to 131071
- receiver_cell: int32 [8, 2048], P(('grp', 'shot')), parts along dimension 0, may hold values from 0 to 131071
- observed: float32 [8, 2, 2048], P(('grp', 'shot')), parts along dimension 0, may hold values from -18 to 18
Outputs:
- updated_velocity: float32 [16, 128, 128], P(('grp', 'depth'), 'lat', 'shot'), parts along dimension 0
- update_direction: float32 [16, 128, 128], P(('grp', 'depth'), 'lat', 'shot'), parts along dimension 0
There are 2 independent parts, one for each index of `grp`. A program takes and returns all parts, laid end to end along the dimension named above; each array names one. Nothing has to cross between parts.
Inputs may be any that keep to these rules, and one draw needn't show every extreme that they name: `source_cell`: a flattened cell index depth * 128 * 128 + x * 128 + y. `receiver_cell`: flattened cell indices depth * 128 * 128 + x * 128 + y; a cell may repeat.
All inputs are finite; a program needn't handle non-finite values. Where the computation divides by a largest or mean magnitude, that divisor is 1e-20 or more.
Results may differ from a plain program's by a relative error of at most 0.00002.
Values sent between devices are 32-bit elements; how exact they have to be, the bound alone decides.
No kernel may reach another device: no remote copies, remote signals or barrier semaphores. Data moves between devices by JAX's collectives and lax.ppermute only.
A program may use at most 64 MiB of HBM per device.

v0:
```python
import jax
import jax.numpy as jnp
from jax import lax
from jax.sharding import PartitionSpec as P

ITERS = 2
COURANT = 0.1
STEP_SIZE = 0.1
EPSILON = 1e-06
NEIGHBOURS = ((1, 0, 0), (-1, 0, 0), (0, 1, 0), (0, -1, 0), (0, 0, 1), (0, 0, -1))


def with_halo(block, sides, width):
    for axis, dim in sides:
        count = lax.axis_size(axis)
        forward = [(i, i + 1) for i in range(count - 1)]
        backward = [(target, source) for source, target in forward]
        low = lax.ppermute(
            lax.slice_in_dim(block, block.shape[dim] - width, None, axis=dim), axis, forward
        )
        high = lax.ppermute(lax.slice_in_dim(block, 0, width, axis=dim), axis, backward)
        block = jnp.concatenate([low, block, high], axis=dim)
    return block


def laplace(padded, buoy_pad):
    depth_cells = padded.shape[-3] - 2
    row_cells = padded.shape[-2] - 2
    col_cells = padded.shape[-1] - 2
    center_field = padded[..., 1:-1, 1:-1, 1:-1]
    center_buoy = buoy_pad[1:-1, 1:-1, 1:-1]
    summed = jnp.zeros(center_field.shape, jnp.float32)
    for shift_depth, shift_row, shift_col in NEIGHBOURS:
        near_buoy = buoy_pad[
            1 + shift_depth : 1 + shift_depth + depth_cells,
            1 + shift_row : 1 + shift_row + row_cells,
            1 + shift_col : 1 + shift_col + col_cells,
        ]
        near_field = padded[
            ...,
            1 + shift_depth : 1 + shift_depth + depth_cells,
            1 + shift_row : 1 + shift_row + row_cells,
            1 + shift_col : 1 + shift_col + col_cells,
        ]
        summed = summed + 0.5 * (center_buoy + near_buoy) * (near_field - center_field)
    return summed


def shrink(cells_array, cut_cells):
    if cut_cells == 0:
        return cells_array
    return cells_array[..., cut_cells:-cut_cells, cut_cells:-cut_cells, cut_cells:-cut_cells]


def pad_lines(cells_array, cut_cells):
    widths = [(0, 0)] * (cells_array.ndim - 1) + [(cut_cells, cut_cells)]
    return jnp.pad(cells_array, widths)


def local_cells(cells, depth_start, row_start, extents, full_rows, margin):
    depth_cells, row_cells, col_cells = extents
    plane_cells = full_rows * col_cells
    depth_pos = cells // plane_cells - depth_start + margin
    row_pos = cells // col_cells % full_rows - row_start + margin
    col_pos = cells % col_cells + margin
    inside = (
        (depth_pos >= 0)
        & (depth_pos < depth_cells + 2 * margin)
        & (row_pos >= 0)
        & (row_pos < row_cells + 2 * margin)
    )
    local_index = (depth_pos * (row_cells + 2 * margin) + row_pos) * (
        col_cells + 2 * margin
    ) + col_pos
    return (jnp.where(inside, local_index, 0), inside)


def shards(
    fwd_prev,
    fwd_now,
    adj_late,
    adj_last,
    velocity,
    density,
    wavelet,
    source_cell,
    receiver_cell,
    observed,
):
    shot_local, depth_cells, row_cells, col_cells = fwd_now.shape
    extents = (depth_cells, row_cells, col_cells)
    full_rows = row_cells * lax.axis_size("lat")
    depth_start = lax.axis_index("depth") * depth_cells
    row_start = lax.axis_index("lat") * row_cells
    steps_count = wavelet.shape[1]
    shot_rows = jnp.arange(shot_local)[:, None]
    shot_ids = jnp.arange(shot_local)
    buoy_width = 1
    buoy_edge = with_halo(1.0 / density, (("depth", 0), ("lat", 1)), buoy_width)
    buoy_pad = pad_lines(buoy_edge, buoy_width)
    receiver_local, receiver_inside = local_cells(
        receiver_cell, depth_start, row_start, extents, full_rows, 0
    )

    def advance(wave_prev, padded_now, stiff_cut, margin, step_index):
        laplacian = laplace(padded_now, shrink(buoy_pad, buoy_width - margin - 1))
        wave_next = 2.0 * shrink(padded_now, 1) - wave_prev + stiff_cut * laplacian
        source_local, source_inside = local_cells(
            source_cell, depth_start, row_start, extents, full_rows, margin
        )
        amount = jnp.where(source_inside, wavelet[:, step_index], 0.0)
        flattened = wave_next.reshape(shot_local, -1).at[shot_ids, source_local].add(amount)
        return (laplacian, flattened.reshape(wave_next.shape))

    def sample(interior, step_index):
        predicted = jnp.take_along_axis(interior.reshape(shot_local, -1), receiver_local, axis=1)
        return predicted - observed[:, step_index, :]

    def forward(stiffness, scaled_first):
        laplacians = []
        misfits = []
        wave_prev = fwd_prev
        wave_now = fwd_now
        for step_index in range(steps_count):
            if step_index == 0:
                padded = with_halo(wave_now, (("depth", 1), ("lat", 2)), 1)
                padded = pad_lines(padded, 1)
            else:
                padded = with_halo(wave_now, (("depth", 1), ("lat", 2)), 1)
                padded = pad_lines(padded, 1)
            laplacian, wave_next = advance(wave_prev, padded, stiffness, 0, step_index)
            laplacians.append(laplacian)
            misfits.append(sample(wave_next, step_index))
            wave_prev, wave_now = (wave_now, wave_next)
        return (laplacians, misfits, scaled_first)

    own_width = velocity.shape[2]
    own_start = lax.axis_index("shot") * own_width
    own_velocity = velocity
    direction = jnp.zeros(velocity.shape, jnp.float32)
    full_velocity = lax.all_gather(velocity, "shot", axis=2, tiled=True)
    for update_index in range(ITERS):
        stiffness = (full_velocity * COURANT) ** 2 * density
        scaled_first = stiffness * adj_last
        laplacians, misfits, adjoint_pad = forward(stiffness, scaled_first)
        gradient = jnp.zeros(extents, jnp.float32)
        late_adj = adj_late
        last_adj = adj_last
        for adjoint_step_index in reversed(range(steps_count)):
            if adjoint_step_index == steps_count - 1:
                adjoint_padded = with_halo(stiffness * last_adj, (("depth", 1), ("lat", 2)), 1)
                adjoint_padded = pad_lines(adjoint_padded, 1)
            else:
                adjoint_padded = with_halo(stiffness * last_adj, (("depth", 1), ("lat", 2)), 1)
                adjoint_padded = pad_lines(adjoint_padded, 1)
            adj_next = (
                2.0 * last_adj
                - late_adj
                + laplace(adjoint_padded, shrink(buoy_pad, buoy_width - 1))
            )
            adjoint_amount = jnp.where(receiver_inside, misfits[adjoint_step_index], 0.0)
            adj_next = (
                adj_next.reshape(shot_local, -1)
                .at[shot_rows, receiver_local]
                .add(adjoint_amount)
                .reshape(last_adj.shape)
            )
            gradient = gradient + jnp.sum(
                adj_next * stiffness * laplacians[adjoint_step_index], axis=0
            )
            late_adj, last_adj = (last_adj, adj_next)
        summed = lax.psum(gradient, "shot")
        largest = lax.pmax(jnp.max(jnp.abs(summed)), ("depth", "lat"))
        whole_direction = summed / (largest + EPSILON)
        full_velocity = full_velocity * jnp.exp(-STEP_SIZE * whole_direction)
        direction = lax.dynamic_slice_in_dim(whole_direction, own_start, own_width, 2)
        own_velocity = lax.dynamic_slice_in_dim(full_velocity, own_start, own_width, 2)
    return (own_velocity, direction)


def solution(mesh):
    placed = (
        P(("grp", "shot"), "depth", "lat", None),
        P(("grp", "shot"), "depth", "lat", None),
        P(("grp", "shot"), "depth", "lat", None),
        P(("grp", "shot"), "depth", "lat", None),
        P(("grp", "depth"), "lat", "shot"),
        P(("grp", "depth"), "lat", None),
        P(("grp", "shot"), None),
        P(("grp", "shot")),
        P(("grp", "shot"), None),
        P(("grp", "shot"), None, None),
    )
    return jax.shard_map(
        shards,
        mesh=mesh,
        in_specs=placed,
        out_specs=(P(("grp", "depth"), "lat", "shot"), P(("grp", "depth"), "lat", "shot")),
        check_vma=False,
    )
```

profile of v0, /device:TPU:0, one launch (start us, length us, event | category | flops | bytes accessed | tf_op | source)
XLA Modules:
  0.0 448.2 jit_solution(14772146906799206289)
XLA Ops:
  7.3 0.9 broadcast_divide_fusion.1
  8.1 1.3 collective-permute-start
  9.4 5.6 %collective-permute-start.2 = (f32[1,64,128]{2,1,0:T(8,128)S(1)}, f32[1,64,128]{2,1,0:T(8,128)S(1)}, u32[]{:S(2)}, u32[]{:S(2)}) collective-permute-start(f32[1,64,128]{2,1,0:T(8,128)S(1)} %get-tuple-element.69), channel_id=1, source_target_pairs={{0,4},{4,8},{8,12},{1,5},{5,9},{9,13},{2,6},{6,10},{10,14},{3,7},{... | collective-permute-start | bytes 98312 | tf_op jit(solution)/shard_map/ppermute | solution.py:18
  15.0 0.9 fusion.158
  15.9 3.9 collective-permute-start.9
  19.9 1.3 collective-permute-start.8
  21.2 1.0 slice_reduce_fusion
  22.1 0.9 fusion.129
  23.5 1.3 collective-permute-start.4
  24.8 3.0 collective-permute-start.6
  27.9 4.9 %all_gather.3 = f32[2,64,128]{1,0,2:T(2,128)S(1)} all-gather(f32[2,64,64]{1,0,2:T(2,128)S(1)} %copy.22), channel_id=1, replica_groups=mesh['grp'=2,'depth'=4,'shot'=2,'lat'=2] {'shot'}, dimensions={2}, use_global_device_ids=true | all-gather | bytes 98304 | tf_op jit(solution)/shard_map/all_gather | solution.py:141
  33.8 1.3 collective-permute-start.1
  35.1 5.2 %collective-permute-start.3 = (f32[2,1,64,128]{3,2,1,0:T(8,128)S(1)}, f32[2,1,64,128]{3,2,1,0:T(8,128)S(1)}, u32[]{:S(2)}, u32[]{:S(2)}) collective-permute-start(f32[2,1,64,128]{3,2,1,0:T(8,128)S(1)} %get-tuple-element.54), channel_id=1, source_target_pairs={{0,4},{4,8},{8,12},{1,5},{5,9},{9,13},{2,6},{6,10},{10,14},{3,7},{... | collective-permute-start | bytes 196616 | tf_op jit(solution)/shard_map/ppermute | solution.py:18
  40.3 1.3 collective-permute-start.10
  41.7 3.2 collective-permute-start.11
  44.9 0.8 collective-permute-done.11
  46.2 0.6 scatter_fusion
  46.8 3.9 collective-permute-start.13
  50.8 1.3 collective-permute-start.12
  52.1 34.9 %gather_fusion.1 = f32[4096]{0:T(1024)S(1)} fusion(f32[2,16384]{1,0:T(2,128)S(1)} %scatter_fusion, s32[4096]{0:T(1024)S(1)} %bitcast.81), kind=kCustom, calls=%fused_computation.1.clone | custom fusion | bytes 65536 | tf_op jit(solution)/shard_map/jit(take_along_axis)/gather | solution.py:116
  87.0 1.3 collective-permute-start.5
  88.3 3.0 collective-permute-start.7
  91.4 0.7 collective-permute-done.7
  92.5 1.3 collective-permute-start.14
  93.8 3.0 collective-permute-start.15
  98.2 0.6 scatter_fusion.1
  98.8 34.9 %gather_fusion = f32[4096]{0:T(1024)S(1)} fusion(f32[2,16384]{1,0:T(2,128)S(1)} %scatter_fusion.1, s32[4096]{0:T(1024)S(1)} %bitcast.82), kind=kCustom, calls=%fused_computation.clone | custom fusion | bytes 65536 | tf_op jit(solution)/shard_map/jit(take_along_axis)/gather | solution.py:116
  133.7 25.9 %scatter_fusion.4 = f32[32768]{0:T(1024)S(1)} fusion(f32[32768]{0:T(1024)S(1)} %bitcast.91, s32[4096]{0:T(1024)S(1)} %bitcast.111, f32[4096]{0:T(1024)S(1)} %bitcast.120), kind=kCustom, calls=%fused_computation.8 | custom fusion | flops 4096 | bytes 65536
  159.6 1.3 collective-permute-start.16
  160.9 5.2 %collective-permute-start.17 = (f32[2,1,64,128]{3,2,1,0:T(8,128)S(1)}, f32[2,1,64,128]{3,2,1,0:T(8,128)S(1)}, u32[]{:S(2)}, u32[]{:S(2)}) collective-permute-start(f32[2,1,64,128]{3,2,1,0:T(8,128)S(1)} %get-tuple-element.52), channel_id=1, source_target_pairs={{0,4},{4,8},{8,12},{1,5},{5,9},{9,13},{2,6},{6,10},{10,14},{3,7},{... | collective-permute-start | bytes 196616 | tf_op jit(solution)/shard_map/ppermute | solution.py:18
  166.2 0.9 collective-permute-done.16
  167.1 1.2 collective-permute-done.17
  168.2 1.3 collective-permute-start.18
  169.5 3.0 collective-permute-start.19
  172.6 0.8 collective-permute-done.19
  173.8 25.9 %scatter_fusion.5 = f32[32768]{0:T(1024)S(1)} fusion(f32[32768]{0:T(1024)S(1)} %bitcast.99, s32[4096]{0:T(1024)S(1)} %bitcast.112, f32[4096]{0:T(1024)S(1)} %bitcast.118), kind=kCustom, calls=%fused_computation.9 | custom fusion | flops 4096 | bytes 65536
  200.4 23.3 %all-reduce.11.cloned.1.call-done = f32[2,64,128]{2,1,0:T(8,128)} async-done(((f32[2,64,128]{2,1,0:T(8,128)}), f32[2,64,128]{2,1,0:T(8,128)}) %all-reduce.11.cloned.1.call-update) | async-done | bytes 65552 | tf_op jit(solution)/shard_map/psum | solution.py:172
  223.7 1.4 abs_reduce_fusion.1
  225.1 16.5 %pmax.14 = f32[]{:T(128)} all-reduce(f32[]{:T(128)} %abs_reduce_fusion.1), channel_id=1, replica_groups=mesh['grp'=2,'depth'=4,'shot'=2,'lat'=2] {'depth','lat'}, use_global_device_ids=true, to_apply=%region_8.10 | all-reduce | flops 1 | bytes 8 | tf_op jit(solution)/shard_map/pmax | solution.py:173
  242.3 0.9 multiply_multiply_fusion
  243.3 0.6 scatter_fusion.2
  243.9 34.9 %gather_fusion.3 = f32[4096]{0:T(1024)S(1)} fusion(f32[2,16384]{1,0:T(2,128)S(1)} %scatter_fusion.2, s32[4096]{0:T(1024)S(1)} %bitcast.83), kind=kCustom, calls=%fused_computation.3.clone | custom fusion | bytes 65536 | tf_op jit(solution)/shard_map/jit(take_along_axis)/gather | solution.py:116
  278.8 1.3 collective-permute-start.25
  280.1 1.3 collective-permute-start.24
  281.5 1.3 collective-permute-start.20
  282.8 5.2 %collective-permute-start.21 = (f32[2,1,64,128]{3,2,1,0:T(8,128)S(1)}, f32[2,1,64,128]{3,2,1,0:T(8,128)S(1)}, u32[]{:S(2)}, u32[]{:S(2)}) collective-permute-start(f32[2,1,64,128]{3,2,1,0:T(8,128)S(1)} %get-tuple-element.48), channel_id=1, source_target_pairs={{0,4},{4,8},{8,12},{1,5},{5,9},{9,13},{2,6},{6,10},{10,14},{3,7},{... | collective-permute-start | bytes 196616 | tf_op jit(solution)/shard_map/ppermute | solution.py:18
  288.1 1.3 collective-permute-start.26
  289.4 3.0 collective-permute-start.27
  292.4 1.3 collective-permute-start.22
  293.7 3.0 collective-permute-start.23
  298.0 34.9 %gather_fusion.2 = f32[4096]{0:T(1024)S(1)} fusion(f32[2,16384]{1,0:T(2,128)S(1)} %scatter_fusion.3, s32[4096]{0:T(1024)S(1)} %bitcast.84), kind=kCustom, calls=%fused_computation.2.clone | custom fusion | bytes 65536 | tf_op jit(solution)/shard_map/jit(take_along_axis)/gather | solution.py:116
  333.3 26.0 %scatter_fusion.6 = f32[32768]{0:T(1024)S(1)} fusion(f32[32768]{0:T(1024)S(1)} %bitcast.94, s32[4096]{0:T(1024)S(1)} %bitcast.113, f32[4096]{0:T(1024)S(1)} %bitcast.119), kind=kCustom, calls=%fused_computation.10 | custom fusion | flops 4096 | bytes 65536
  359.4 1.3 collective-permute-start.28
  360.7 4.6 %collective-permute-start.29 = (f32[2,1,64,128]{3,2,1,0:T(8,128)S(1)}, f32[2,1,64,128]{3,2,1,0:T(8,128)S(1)}, u32[]{:S(2)}, u32[]{:S(2)}) collective-permute-start(f32[2,1,64,128]{3,2,1,0:T(8,128)S(1)} %get-tuple-element.46), channel_id=1, source_target_pairs={{0,4},{4,8},{8,12},{1,5},{5,9},{9,13},{2,6},{6,10},{10,14},{3,7},{... | collective-permute-start | bytes 196616 | tf_op jit(solution)/shard_map/ppermute | solution.py:18
  365.6 1.6 collective-permute-done.29
  367.2 1.3 collective-permute-start.30
  368.5 3.0 collective-permute-start.31
  371.6 0.8 collective-permute-done.31
  372.8 25.9 %scatter_fusion.7 = f32[32768]{0:T(1024)S(1)} fusion(f32[32768]{0:T(1024)S(1)} %bitcast.97, s32[4096]{0:T(1024)S(1)} %bitcast.114, f32[4096]{0:T(1024)S(1)} %bitcast.117), kind=kCustom, calls=%fused_computation.11 | custom fusion | flops 4096 | bytes 65536
  399.3 21.8 %all-reduce.13.cloned.1.call-done = f32[2,64,128]{2,1,0:T(8,128)} async-done(((f32[2,64,128]{2,1,0:T(8,128)}), f32[2,64,128]{2,1,0:T(8,128)}) %all-reduce.13.cloned.1.call-update) | async-done | bytes 65552 | tf_op jit(solution)/shard_map/psum | solution.py:172
  421.1 1.4 abs_reduce_fusion
  422.6 16.5 %pmax.15 = f32[]{:T(128)} all-reduce(f32[]{:T(128)} %abs_reduce_fusion), channel_id=1, replica_groups=mesh['grp'=2,'depth'=4,'shot'=2,'lat'=2] {'depth','lat'}, use_global_device_ids=true, to_apply=%region_17.19 | all-reduce | flops 1 | bytes 8 | tf_op jit(solution)/shard_map/pmax | solution.py:173
  439.7 0.9 broadcast_divide_fusion
  440.6 0.7 dynamic-slice_multiply_fusion
  (128 shorter events, 8.1 us)
Async XLA Ops:
  7.2 15.9 %copy-start.9 = (s32[2]{0:T(128)S(1)}, s32[2]{0:T(128)}, u32[]{:S(2)}) copy-start(s32[2]{0:T(128)} %constant.190) | copy-start | bytes 28
  7.2 16.0 %copy-start.8 = (s32[2]{0:T(128)S(1)}, s32[2]{0:T(128)}, u32[]{:S(2)}) copy-start(s32[2]{0:T(128)} %constant.187) | copy-start | bytes 28
  7.2 16.1 %copy-start.6 = (f32[2,2,2048]{2,1,0:T(2,128)S(1)}, f32[2,2,2048]{2,1,0:T(2,128)}, u32[]{:S(2)}) copy-start(f32[2,2,2048]{2,1,0:T(2,128)} %param.21) | copy-start | bytes 98308
  7.2 16.1 %copy-start.7 = (s32[2]{0:T(128)S(1)}, s32[2]{0:T(128)}, u32[]{:S(2)}) copy-start(s32[2]{0:T(128)} %param.19) | copy-start | bytes 28
  7.2 16.2 %copy-start.5 = (f32[2,64,64]{2,1,0:T(8,128)S(1)}, f32[2,64,64]{2,1,0:T(8,128)}, u32[]{:S(2)}) copy-start(f32[2,64,64]{2,1,0:T(8,128)} %param.16) | copy-start | bytes 98308
  7.2 216.4 %all-reduce.11.cloned.1.call-start = ((), (), s32[]{:S(2)}) async-start(), calls=%async_computation | async-start | bytes 131072 | tf_op jit(solution)/shard_map/psum | solution.py:172
  8.1 15.4 %collective-permute-start = (f32[1,64,128]{2,1,0:T(8,128)S(1)}, f32[1,64,128]{2,1,0:T(8,128)S(1)}, u32[]{:S(2)}, u32[]{:S(2)}) collective-permute-start(f32[1,64,128]{2,1,0:T(8,128)S(1)} %get-tuple-element.70), channel_id=1, source_target_pairs={{4,0},{8,4},{12,8},{5,1},{9,5},{13,9},{6,2},{10,6},{14,10},{7,3},{... | collective-permute-start | bytes 98312 | tf_op jit(solution)/shard_map/ppermute | solution.py:21
  9.4 14.1 %collective-permute-start.2 = (f32[1,64,128]{2,1,0:T(8,128)S(1)}, f32[1,64,128]{2,1,0:T(8,128)S(1)}, u32[]{:S(2)}, u32[]{:S(2)}) collective-permute-start(f32[1,64,128]{2,1,0:T(8,128)S(1)} %get-tuple-element.69), channel_id=1, source_target_pairs={{0,4},{4,8},{8,12},{1,5},{5,9},{9,13},{2,6},{6,10},{10,14},{3,7},{... | collective-permute-start | bytes 98312 | tf_op jit(solution)/shard_map/ppermute | solution.py:18
  15.9 24.3 %collective-permute-start.9 = (f32[2,1,64,128]{3,2,1,0:T(8,128)S(1)}, f32[2,1,64,128]{3,2,1,0:T(8,128)S(1)}, u32[]{:S(2)}, u32[]{:S(2)}) collective-permute-start(f32[2,1,64,128]{3,2,1,0:T(8,128)S(1)} %get-tuple-element.63), channel_id=1, source_target_pairs={{0,4},{4,8},{8,12},{1,5},{5,9},{9,13},{2,6},{6,10},{10,14},{3,7},{... | collective-permute-start | bytes 196616 | tf_op jit(solution)/shard_map/ppermute | solution.py:18
  19.9 20.4 %collective-permute-start.8 = (f32[2,1,64,128]{3,2,1,0:T(8,128)S(1)}, f32[2,1,64,128]{3,2,1,0:T(8,128)S(1)}, u32[]{:S(2)}, u32[]{:S(2)}) collective-permute-start(f32[2,1,64,128]{3,2,1,0:T(8,128)S(1)} %get-tuple-element.62), channel_id=1, source_target_pairs={{4,0},{8,4},{12,8},{5,1},{9,5},{13,9},{6,2},{10,6},{14,10},{7,3},{... | collective-permute-start | bytes 196616 | tf_op jit(solution)/shard_map/ppermute | solution.py:21
  23.4 9.8 %copy-start.2 = (f32[2,64,128]{2,1,0:T(8,128)S(1)}, f32[2,64,128]{2,1,0:T(8,128)}, u32[]{:S(2)}) copy-start(f32[2,64,128]{2,1,0:T(8,128)} %param.17) | copy-start | bytes 196612
  23.5 9.4 %collective-permute-start.4 = (f32[4,1,128]{2,1,0:T(1,128)S(1)}, f32[4,1,128]{2,1,0:T(1,128)S(1)}, u32[]{:S(2)}, u32[]{:S(2)}) collective-permute-start(f32[4,1,128]{2,1,0:T(1,128)S(1)} %get-tuple-element.61), channel_id=1, source_target_pairs={{1,0},{3,2},{5,4},{7,6},{9,8},{11,10},{13,12},{15,14},{17,16},{19,... | collective-permute-start | bytes 6152 | tf_op jit(solution)/shard_map/ppermute | solution.py:21
  24.8 8.1 %collective-permute-start.6 = (f32[4,1,128]{2,1,0:T(1,128)S(1)}, f32[4,1,128]{2,1,0:T(1,128)S(1)}, u32[]{:S(2)}, u32[]{:S(2)}) collective-permute-start(f32[4,1,128]{2,1,0:T(1,128)S(1)} %get-tuple-element.60), channel_id=1, source_target_pairs={{0,1},{2,3},{4,5},{6,7},{8,9},{10,11},{12,13},{14,15},{16,17},{18,... | collective-permute-start | bytes 6152 | tf_op jit(solution)/shard_map/ppermute | solution.py:18
  32.8 0.9 copy-start.1
  33.1 7.1 %copy-start = (f32[2,2,64,128]{3,2,1,0:T(8,128)S(1)}, f32[2,2,64,128]{3,2,1,0:T(8,128)}, u32[]{:S(2)}) copy-start(f32[2,2,64,128]{3,2,1,0:T(8,128)} %param.13) | copy-start | bytes 393220
  33.8 53.2 %collective-permute-start.1 = (f32[2,1,64,128]{3,2,1,0:T(8,128)S(1)}, f32[2,1,64,128]{3,2,1,0:T(8,128)S(1)}, u32[]{:S(2)}, u32[]{:S(2)}) collective-permute-start(f32[2,1,64,128]{3,2,1,0:T(8,128)S(1)} %get-tuple-element.55), channel_id=1, source_target_pairs={{4,0},{8,4},{12,8},{5,1},{9,5},{13,9},{6,2},{10,6},{14,10},{7,3},{... | collective-permute-start | bytes 196616 | tf_op jit(solution)/shard_map/ppermute | solution.py:21
  35.1 51.9 %collective-permute-start.3 = (f32[2,1,64,128]{3,2,1,0:T(8,128)S(1)}, f32[2,1,64,128]{3,2,1,0:T(8,128)S(1)}, u32[]{:S(2)}, u32[]{:S(2)}) collective-permute-start(f32[2,1,64,128]{3,2,1,0:T(8,128)S(1)} %get-tuple-element.54), channel_id=1, source_target_pairs={{0,4},{4,8},{8,12},{1,5},{5,9},{9,13},{2,6},{6,10},{10,14},{3,7},{... | collective-permute-start | bytes 196616 | tf_op jit(solution)/shard_map/ppermute | solution.py:18
  40.3 4.5 %collective-permute-start.10 = (f32[2,4,1,128]{3,2,1,0:T(1,128)S(1)}, f32[2,4,1,128]{3,2,1,0:T(1,128)S(1)}, u32[]{:S(2)}, u32[]{:S(2)}) collective-permute-start(f32[2,4,1,128]{3,2,1,0:T(1,128)S(1)} %get-tuple-element.45), channel_id=1, source_target_pairs={{1,0},{3,2},{5,4},{7,6},{9,8},{11,10},{13,12},{15,14},{17,16},{19,... | collective-permute-start | bytes 12296 | tf_op jit(solution)/shard_map/ppermute | solution.py:21
  41.6 4.2 copy-start.4
  41.7 4.0 collective-permute-start.11
  46.8 45.6 %collective-permute-start.13 = (f32[2,1,64,128]{3,2,1,0:T(8,128)S(1)}, f32[2,1,64,128]{3,2,1,0:T(8,128)S(1)}, u32[]{:S(2)}, u32[]{:S(2)}) collective-permute-start(f32[2,1,64,128]{3,2,1,0:T(8,128)S(1)} %get-tuple-element.57), channel_id=1, source_target_pairs={{0,4},{4,8},{8,12},{1,5},{5,9},{9,13},{2,6},{6,10},{10,14},{3,7},{... | collective-permute-start | bytes 196616 | tf_op jit(solution)/shard_map/ppermute | solution.py:18
  50.8 41.7 %collective-permute-start.12 = (f32[2,1,64,128]{3,2,1,0:T(8,128)S(1)}, f32[2,1,64,128]{3,2,1,0:T(8,128)S(1)}, u32[]{:S(2)}, u32[]{:S(2)}) collective-permute-start(f32[2,1,64,128]{3,2,1,0:T(8,128)S(1)} %get-tuple-element.56), channel_id=1, source_target_pairs={{4,0},{8,4},{12,8},{5,1},{9,5},{13,9},{6,2},{10,6},{14,10},{7,3},{... | collective-permute-start | bytes 196616 | tf_op jit(solution)/shard_map/ppermute | solution.py:21
  87.0 4.4 collective-permute-start.5
  88.3 3.8 collective-permute-start.7
  91.4 5.4 %copy-start.3 = (f32[2,2,64,128]{3,2,1,0:T(8,128)S(1)}, f32[2,2,64,128]{3,2,1,0:T(8,128)}, u32[]{:S(2)}) copy-start(f32[2,2,64,128]{3,2,1,0:T(8,128)} %param.14) | copy-start | bytes 393220
  92.5 4.5 %collective-permute-start.14 = (f32[2,4,1,128]{3,2,1,0:T(1,128)S(1)}, f32[2,4,1,128]{3,2,1,0:T(1,128)S(1)}, u32[]{:S(2)}, u32[]{:S(2)}) collective-permute-start(f32[2,4,1,128]{3,2,1,0:T(1,128)S(1)} %get-tuple-element.43), channel_id=1, source_target_pairs={{1,0},{3,2},{5,4},{7,6},{9,8},{11,10},{13,12},{15,14},{17,16},{19,... | collective-permute-start | bytes 12296 | tf_op jit(solution)/shard_map/ppermute | solution.py:21
  93.8 3.8 collective-permute-start.15
  159.6 7.4 %collective-permute-start.16 = (f32[2,1,64,128]{3,2,1,0:T(8,128)S(1)}, f32[2,1,64,128]{3,2,1,0:T(8,128)S(1)}, u32[]{:S(2)}, u32[]{:S(2)}) collective-permute-start(f32[2,1,64,128]{3,2,1,0:T(8,128)S(1)} %get-tuple-element.53), channel_id=1, source_target_pairs={{4,0},{8,4},{12,8},{5,1},{9,5},{13,9},{6,2},{10,6},{14,10},{7,3},{... | collective-permute-start | bytes 196616 | tf_op jit(solution)/shard_map/ppermute | solution.py:21
  160.9 7.3 %collective-permute-start.17 = (f32[2,1,64,128]{3,2,1,0:T(8,128)S(1)}, f32[2,1,64,128]{3,2,1,0:T(8,128)S(1)}, u32[]{:S(2)}, u32[]{:S(2)}) collective-permute-start(f32[2,1,64,128]{3,2,1,0:T(8,128)S(1)} %get-tuple-element.52), channel_id=1, source_target_pairs={{0,4},{4,8},{8,12},{1,5},{5,9},{9,13},{2,6},{6,10},{10,14},{3,7},{... | collective-permute-start | bytes 196616 | tf_op jit(solution)/shard_map/ppermute | solution.py:18
  168.2 4.3 collective-permute-start.18
  169.5 3.8 collective-permute-start.19
  200.3 220.8 %all-reduce.13.cloned.1.call-start = ((), (), s32[]{:S(2)}) async-start(), calls=%async_computation.1 | async-start | bytes 131072 | tf_op jit(solution)/shard_map/psum | solution.py:172
  278.8 9.1 %collective-permute-start.25 = (f32[2,1,64,128]{3,2,1,0:T(8,128)S(1)}, f32[2,1,64,128]{3,2,1,0:T(8,128)S(1)}, u32[]{:S(2)}, u32[]{:S(2)}) collective-permute-start(f32[2,1,64,128]{3,2,1,0:T(8,128)S(1)} %get-tuple-element.51), channel_id=1, source_target_pairs={{0,4},{4,8},{8,12},{1,5},{5,9},{9,13},{2,6},{6,10},{10,14},{3,7},{... | collective-permute-start | bytes 196616 | tf_op jit(solution)/shard_map/ppermute | solution.py:18
  280.1 7.9 %collective-permute-start.24 = (f32[2,1,64,128]{3,2,1,0:T(8,128)S(1)}, f32[2,1,64,128]{3,2,1,0:T(8,128)S(1)}, u32[]{:S(2)}, u32[]{:S(2)}) collective-permute-start(f32[2,1,64,128]{3,2,1,0:T(8,128)S(1)} %get-tuple-element.50), channel_id=1, source_target_pairs={{4,0},{8,4},{12,8},{5,1},{9,5},{13,9},{6,2},{10,6},{14,10},{7,3},{... | collective-permute-start | bytes 196616 | tf_op jit(solution)/shard_map/ppermute | solution.py:21
  281.5 10.9 %collective-permute-start.20 = (f32[2,1,64,128]{3,2,1,0:T(8,128)S(1)}, f32[2,1,64,128]{3,2,1,0:T(8,128)S(1)}, u32[]{:S(2)}, u32[]{:S(2)}) collective-permute-start(f32[2,1,64,128]{3,2,1,0:T(8,128)S(1)} %get-tuple-element.49), channel_id=1, source_target_pairs={{4,0},{8,4},{12,8},{5,1},{9,5},{13,9},{6,2},{10,6},{14,10},{7,3},{... | collective-permute-start | bytes 196616 | tf_op jit(solution)/shard_map/ppermute | solution.py:21
  282.8 9.6 %collective-permute-start.21 = (f32[2,1,64,128]{3,2,1,0:T(8,128)S(1)}, f32[2,1,64,128]{3,2,1,0:T(8,128)S(1)}, u32[]{:S(2)}, u32[]{:S(2)}) collective-permute-start(f32[2,1,64,128]{3,2,1,0:T(8,128)S(1)} %get-tuple-element.48), channel_id=1, source_target_pairs={{0,4},{4,8},{8,12},{1,5},{5,9},{9,13},{2,6},{6,10},{10,14},{3,7},{... | collective-permute-start | bytes 196616 | tf_op jit(solution)/shard_map/ppermute | solution.py:18
  288.1 8.7 %collective-permute-start.26 = (f32[2,4,1,128]{3,2,1,0:T(1,128)S(1)}, f32[2,4,1,128]{3,2,1,0:T(1,128)S(1)}, u32[]{:S(2)}, u32[]{:S(2)}) collective-permute-start(f32[2,4,1,128]{3,2,1,0:T(1,128)S(1)} %get-tuple-element.37), channel_id=1, source_target_pairs={{1,0},{3,2},{5,4},{7,6},{9,8},{11,10},{13,12},{15,14},{17,16},{19,... | collective-permute-start | bytes 12296 | tf_op jit(solution)/shard_map/ppermute | solution.py:21
  289.4 7.4 %collective-permute-start.27 = (f32[2,4,1,128]{3,2,1,0:T(1,128)S(1)}, f32[2,4,1,128]{3,2,1,0:T(1,128)S(1)}, u32[]{:S(2)}, u32[]{:S(2)}) collective-permute-start(f32[2,4,1,128]{3,2,1,0:T(1,128)S(1)} %get-tuple-element.36), channel_id=1, source_target_pairs={{0,1},{2,3},{4,5},{6,7},{8,9},{10,11},{12,13},{14,15},{16,17},{18,... | collective-permute-start | bytes 12296 | tf_op jit(solution)/shard_map/ppermute | solution.py:18
  292.4 40.5 %collective-permute-start.22 = (f32[2,4,1,128]{3,2,1,0:T(1,128)S(1)}, f32[2,4,1,128]{3,2,1,0:T(1,128)S(1)}, u32[]{:S(2)}, u32[]{:S(2)}) collective-permute-start(f32[2,4,1,128]{3,2,1,0:T(1,128)S(1)} %get-tuple-element.35), channel_id=1, source_target_pairs={{1,0},{3,2},{5,4},{7,6},{9,8},{11,10},{13,12},{15,14},{17,16},{19,... | collective-permute-start | bytes 12296 | tf_op jit(solution)/shard_map/ppermute | solution.py:21
  293.7 39.2 %collective-permute-start.23 = (f32[2,4,1,128]{3,2,1,0:T(1,128)S(1)}, f32[2,4,1,128]{3,2,1,0:T(1,128)S(1)}, u32[]{:S(2)}, u32[]{:S(2)}) collective-permute-start(f32[2,4,1,128]{3,2,1,0:T(1,128)S(1)} %get-tuple-element.34), channel_id=1, source_target_pairs={{0,1},{2,3},{4,5},{6,7},{8,9},{10,11},{12,13},{14,15},{16,17},{18,... | collective-permute-start | bytes 12296 | tf_op jit(solution)/shard_map/ppermute | solution.py:18
  359.4 6.2 %collective-permute-start.28 = (f32[2,1,64,128]{3,2,1,0:T(8,128)S(1)}, f32[2,1,64,128]{3,2,1,0:T(8,128)S(1)}, u32[]{:S(2)}, u32[]{:S(2)}) collective-permute-start(f32[2,1,64,128]{3,2,1,0:T(8,128)S(1)} %get-tuple-element.47), channel_id=1, source_target_pairs={{4,0},{8,4},{12,8},{5,1},{9,5},{13,9},{6,2},{10,6},{14,10},{7,3},{... | collective-permute-start | bytes 196616 | tf_op jit(solution)/shard_map/ppermute | solution.py:21
  360.7 6.5 %collective-permute-start.29 = (f32[2,1,64,128]{3,2,1,0:T(8,128)S(1)}, f32[2,1,64,128]{3,2,1,0:T(8,128)S(1)}, u32[]{:S(2)}, u32[]{:S(2)}) collective-permute-start(f32[2,1,64,128]{3,2,1,0:T(8,128)S(1)} %get-tuple-element.46), channel_id=1, source_target_pairs={{0,4},{4,8},{8,12},{1,5},{5,9},{9,13},{2,6},{6,10},{10,14},{3,7},{... | collective-permute-start | bytes 196616 | tf_op jit(solution)/shard_map/ppermute | solution.py:18
  367.2 4.3 collective-permute-start.30
  368.5 3.8 collective-permute-start.31
Sparse Core Ops, SparseCore 0:
  200.5 23.1 all-reduce.10
  399.5 21.6 all-reduce.12
where the time goes:
time: 449 us; the launch traced here: 448 us
  local copies, waits for them, and re-layouts  143 us (32%)
  other arithmetic  118 us (26%)
  starting transfers between devices  80 us (18%)
  waiting for transfers between devices  52.8 us (12%)
  blocking collectives  38 us (8%)
  between operations  16.5 us (4%)
    gather x8, local copies, waits for them, and re-layouts, sample(): jnp.take_along_axis(interior.reshape(shot_local, -1), receiver_local, axi...  139 us
    unnamed x11, other arithmetic  105 us
    ppermute x16, starting transfers between devices, with_halo(): lax.ppermute(lax.slice_in_dim(block, block.shape[dim] - width, None, axis...  59.3 us
    psum x2, waiting for transfers between devices, shards(): summed = lax.psum(gradient, 'shot')  45.1 us
    pmax x2, blocking collectives, shards(): largest = lax.pmax(jnp.max(jnp.abs(summed)), ('depth', 'lat'))  33 us
    ppermute x16, starting transfers between devices, with_halo(): lax.ppermute(lax.slice_in_dim(block, 0, width, axis=dim), axis, backward)  20.6 us
  transfers between devices with their start and end apart: 34, of which 11 were waited for; matrix products, arithmetic and copies ran while one was open for 17% of the time, Pallas kernels for 0%

commit v1 on v0

--- a/solution.py
+++ b/solution.py
@@ -169,7 +169,7 @@
                 adj_next * stiffness * laplacians[adjoint_step_index], axis=0
             )
             late_adj, last_adj = (last_adj, adj_next)
-        summed = lax.psum(gradient, "shot")
+        summed = jnp.sum(lax.all_gather(gradient, "shot"), axis=0)
         largest = lax.pmax(jnp.max(jnp.abs(summed)), ("depth", "lat"))
         whole_direction = summed / (largest + EPSILON)
         full_velocity = full_velocity * jnp.exp(-STEP_SIZE * whole_direction)

time: 449 us -> 397 us (0.88)
  waiting for transfers between devices: 52.8 us -> 7.69 us
  between operations: 16.5 us -> 3.12 us
  blocking collectives: 38 us -> 48.8 us
    psum x2 -> x0, waiting for transfers between devices: 45.1 us -> none  [shards(): summed = lax.psum(gradient, 'shot')]
    all_gather x0 -> x2, blocking collectives: none -> 10.1 us  [shards(): summed = jnp.sum(lax.all_gather(gradient, 'shot'), axis=0)]
  transfers between devices with their start and end apart: 34 -> 32, of which waited for: 11 -> 9; matrix products, arithmetic and copies ran while one was open for 17% -> 19% of each run, Pallas kernels for 0% -> 0%
where the time goes in v1:
time: 397 us; the launch traced here: 396 us
  local copies, waits for them, and re-layouts  143 us (36%)
  other arithmetic  114 us (29%)
  starting transfers between devices  79.9 us (20%)
  blocking collectives  48.8 us (12%)
  waiting for transfers between devices  7.69 us (2%)
    gather x8, local copies, waits for them, and re-layouts, sample(): jnp.take_along_axis(interior.reshape(shot_local, -1), receiver_local, axi...  139 us
    unnamed x11, other arithmetic  105 us
    ppermute x16, starting transfers between devices, with_halo(): lax.ppermute(lax.slice_in_dim(block, block.shape[dim] - width, None, axis...  59.3 us
    pmax x2, blocking collectives, shards(): largest = lax.pmax(jnp.max(jnp.abs(summed)), ('depth', 'lat'))  33.8 us
    ppermute x16, starting transfers between devices, with_halo(): lax.ppermute(lax.slice_in_dim(block, 0, width, axis=dim), axis, backward)  20.6 us
    all_gather x2, blocking collectives, shards(): summed = jnp.sum(lax.all_gather(gradient, 'shot'), axis=0)  10.1 us
  transfers between devices with their start and end apart: 32, of which 9 were waited for; matrix products, arithmetic and copies ran while one was open for 19% of the time, Pallas kernels for 0%

profile of v1, /device:TPU:0, one launch (start us, length us, event | category | flops | bytes accessed | tf_op | source)
XLA Modules:
  0.0 395.9 jit_solution(13644459006873749577)
XLA Ops:
  0.7 0.9 broadcast_divide_fusion.1
  1.6 1.3 collective-permute-start
  2.9 5.6 %collective-permute-start.2 = (f32[1,64,128]{2,1,0:T(8,128)S(1)}, f32[1,64,128]{2,1,0:T(8,128)S(1)}, u32[]{:S(2)}, u32[]{:S(2)}) collective-permute-start(f32[1,64,128]{2,1,0:T(8,128)S(1)} %get-tuple-element.69), channel_id=1, source_target_pairs={{0,4},{4,8},{8,12},{1,5},{5,9},{9,13},{2,6},{6,10},{10,14},{3,7},{... | collective-permute-start | bytes 98312 | tf_op jit(solution)/shard_map/ppermute | solution.py:18
  8.5 0.9 fusion.158
  9.4 3.9 collective-permute-start.9
  13.3 1.3 collective-permute-start.8
  14.6 1.0 slice_reduce_fusion
  15.6 0.9 fusion.129
  17.0 1.3 collective-permute-start.4
  18.3 3.0 collective-permute-start.6
  21.3 4.9 %all_gather.11 = f32[2,64,128]{1,0,2:T(2,128)S(1)} all-gather(f32[2,64,64]{1,0,2:T(2,128)S(1)} %copy.22), channel_id=1, replica_groups=mesh['grp'=2,'depth'=4,'shot'=2,'lat'=2] {'shot'}, dimensions={2}, use_global_device_ids=true | all-gather | bytes 98304 | tf_op jit(solution)/shard_map/all_gather | solution.py:141
  27.2 1.3 collective-permute-start.1
  28.5 5.2 %collective-permute-start.3 = (f32[2,1,64,128]{3,2,1,0:T(8,128)S(1)}, f32[2,1,64,128]{3,2,1,0:T(8,128)S(1)}, u32[]{:S(2)}, u32[]{:S(2)}) collective-permute-start(f32[2,1,64,128]{3,2,1,0:T(8,128)S(1)} %get-tuple-element.54), channel_id=1, source_target_pairs={{0,4},{4,8},{8,12},{1,5},{5,9},{9,13},{2,6},{6,10},{10,14},{3,7},{... | collective-permute-start | bytes 196616 | tf_op jit(solution)/shard_map/ppermute | solution.py:18
  33.8 1.3 collective-permute-start.10
  35.1 3.2 collective-permute-start.11
  38.3 0.8 collective-permute-done.11
  39.6 0.6 scatter_fusion
  40.3 3.9 collective-permute-start.13
  44.2 1.3 collective-permute-start.12
  45.5 34.9 %gather_fusion.1 = f32[4096]{0:T(1024)S(1)} fusion(f32[2,16384]{1,0:T(2,128)S(1)} %scatter_fusion, s32[4096]{0:T(1024)S(1)} %bitcast.83), kind=kCustom, calls=%fused_computation.1.clone | custom fusion | bytes 65536 | tf_op jit(solution)/shard_map/jit(take_along_axis)/gather | solution.py:116
  80.4 1.3 collective-permute-start.5
  81.7 3.0 collective-permute-start.7
  84.8 0.7 collective-permute-done.7
  85.9 1.3 collective-permute-start.14
  87.2 3.0 collective-permute-start.15
  90.4 0.6 collective-permute-done.15
  91.6 0.6 scatter_fusion.1
  92.2 34.9 %gather_fusion = f32[4096]{0:T(1024)S(1)} fusion(f32[2,16384]{1,0:T(2,128)S(1)} %scatter_fusion.1, s32[4096]{0:T(1024)S(1)} %bitcast.84), kind=kCustom, calls=%fused_computation.clone | custom fusion | bytes 65536 | tf_op jit(solution)/shard_map/jit(take_along_axis)/gather | solution.py:116
  127.2 25.9 %scatter_fusion.4 = f32[32768]{0:T(1024)S(1)} fusion(f32[32768]{0:T(1024)S(1)} %bitcast.93, s32[4096]{0:T(1024)S(1)} %bitcast.115, f32[4096]{0:T(1024)S(1)} %bitcast.124), kind=kCustom, calls=%fused_computation.8 | custom fusion | flops 4096 | bytes 65536
  153.1 1.3 collective-permute-start.16
  154.4 5.2 %collective-permute-start.17 = (f32[2,1,64,128]{3,2,1,0:T(8,128)S(1)}, f32[2,1,64,128]{3,2,1,0:T(8,128)S(1)}, u32[]{:S(2)}, u32[]{:S(2)}) collective-permute-start(f32[2,1,64,128]{3,2,1,0:T(8,128)S(1)} %get-tuple-element.52), channel_id=1, source_target_pairs={{0,4},{4,8},{8,12},{1,5},{5,9},{9,13},{2,6},{6,10},{10,14},{3,7},{... | collective-permute-start | bytes 196616 | tf_op jit(solution)/shard_map/ppermute | solution.py:18
  159.6 0.9 collective-permute-done.16
  160.5 1.2 collective-permute-done.17
  161.7 1.3 collective-permute-start.18
  163.0 3.0 collective-permute-start.19
  166.0 0.8 collective-permute-done.19
  167.2 25.9 %scatter_fusion.5 = f32[32768]{0:T(1024)S(1)} fusion(f32[32768]{0:T(1024)S(1)} %bitcast.101, s32[4096]{0:T(1024)S(1)} %bitcast.116, f32[4096]{0:T(1024)S(1)} %bitcast.122), kind=kCustom, calls=%fused_computation.9 | custom fusion | flops 4096 | bytes 65536
  193.1 5.0 %all-gather = f32[4,64,128]{2,1,0:T(8,128)S(1)} all-gather(f32[2,64,128]{2,1,0:T(8,128)S(1)} %add.382), channel_id=2, replica_groups=mesh['grp'=2,'depth'=4,'shot'=2,'lat'=2] {'shot'}, dimensions={0}, use_global_device_ids=true | all-gather | bytes 196608 | tf_op jit(solution)/shard_map/all_gather | solution.py:172
  198.2 0.6 abs_reduce_fusion.1
  198.8 17.3 %pmax.14 = f32[]{:T(128)} all-reduce(f32[]{:T(128)} %abs_reduce_fusion.1), channel_id=1, replica_groups=mesh['grp'=2,'depth'=4,'shot'=2,'lat'=2] {'depth','lat'}, use_global_device_ids=true, to_apply=%region_8.10 | all-reduce | flops 1 | bytes 8 | tf_op jit(solution)/shard_map/pmax | solution.py:173
  216.9 0.6 scatter_fusion.2
  217.6 34.9 %gather_fusion.3 = f32[4096]{0:T(1024)S(1)} fusion(f32[2,16384]{1,0:T(2,128)S(1)} %scatter_fusion.2, s32[4096]{0:T(1024)S(1)} %bitcast.85), kind=kCustom, calls=%fused_computation.3.clone | custom fusion | bytes 65536 | tf_op jit(solution)/shard_map/jit(take_along_axis)/gather | solution.py:116
  252.5 1.3 collective-permute-start.25
  253.8 1.3 collective-permute-start.24
  255.1 1.3 collective-permute-start.20
  256.4 5.2 %collective-permute-start.21 = (f32[2,1,64,128]{3,2,1,0:T(8,128)S(1)}, f32[2,1,64,128]{3,2,1,0:T(8,128)S(1)}, u32[]{:S(2)}, u32[]{:S(2)}) collective-permute-start(f32[2,1,64,128]{3,2,1,0:T(8,128)S(1)} %get-tuple-element.48), channel_id=1, source_target_pairs={{0,4},{4,8},{8,12},{1,5},{5,9},{9,13},{2,6},{6,10},{10,14},{3,7},{... | collective-permute-start | bytes 196616 | tf_op jit(solution)/shard_map/ppermute | solution.py:18
  261.7 1.3 collective-permute-start.26
  263.0 3.0 collective-permute-start.27
  266.0 1.3 collective-permute-start.22
  267.3 3.0 collective-permute-start.23
  270.9 0.6 scatter_fusion.3
  271.6 34.9 %gather_fusion.2 = f32[4096]{0:T(1024)S(1)} fusion(f32[2,16384]{1,0:T(2,128)S(1)} %scatter_fusion.3, s32[4096]{0:T(1024)S(1)} %bitcast.86), kind=kCustom, calls=%fused_computation.2.clone | custom fusion | bytes 65536 | tf_op jit(solution)/shard_map/jit(take_along_axis)/gather | solution.py:116
  306.9 26.0 %scatter_fusion.6 = f32[32768]{0:T(1024)S(1)} fusion(f32[32768]{0:T(1024)S(1)} %bitcast.96, s32[4096]{0:T(1024)S(1)} %bitcast.117, f32[4096]{0:T(1024)S(1)} %bitcast.123), kind=kCustom, calls=%fused_computation.10 | custom fusion | flops 4096 | bytes 65536
  333.0 1.3 collective-permute-start.28
  334.3 4.6 %collective-permute-start.29 = (f32[2,1,64,128]{3,2,1,0:T(8,128)S(1)}, f32[2,1,64,128]{3,2,1,0:T(8,128)S(1)}, u32[]{:S(2)}, u32[]{:S(2)}) collective-permute-start(f32[2,1,64,128]{3,2,1,0:T(8,128)S(1)} %get-tuple-element.46), channel_id=1, source_target_pairs={{0,4},{4,8},{8,12},{1,5},{5,9},{9,13},{2,6},{6,10},{10,14},{3,7},{... | collective-permute-start | bytes 196616 | tf_op jit(solution)/shard_map/ppermute | solution.py:18
  339.3 1.6 collective-permute-done.29
  340.9 1.3 collective-permute-start.30
  342.1 3.0 collective-permute-start.31
  345.2 0.8 collective-permute-done.31
  346.4 25.9 %scatter_fusion.7 = f32[32768]{0:T(1024)S(1)} fusion(f32[32768]{0:T(1024)S(1)} %bitcast.99, s32[4096]{0:T(1024)S(1)} %bitcast.118, f32[4096]{0:T(1024)S(1)} %bitcast.121), kind=kCustom, calls=%fused_computation.11 | custom fusion | flops 4096 | bytes 65536
  372.3 5.1 %all-gather.1 = f32[4,64,128]{2,1,0:T(8,128)S(1)} all-gather(f32[2,64,128]{2,1,0:T(8,128)S(1)} %add.404), channel_id=3, replica_groups=mesh['grp'=2,'depth'=4,'shot'=2,'lat'=2] {'shot'}, dimensions={0}, use_global_device_ids=true | all-gather | bytes 196608 | tf_op jit(solution)/shard_map/all_gather | solution.py:172
  377.4 0.6 abs_reduce_fusion
  378.0 16.5 %pmax.15 = f32[]{:T(128)} all-reduce(f32[]{:T(128)} %abs_reduce_fusion), channel_id=1, replica_groups=mesh['grp'=2,'depth'=4,'shot'=2,'lat'=2] {'depth','lat'}, use_global_device_ids=true, to_apply=%region_17.19 | all-reduce | flops 1 | bytes 8 | tf_op jit(solution)/shard_map/pmax | solution.py:173
  395.2 0.7 dynamic-slice_multiply_fusion
  (126 shorter events, 5.6 us)
Async XLA Ops:
  0.6 15.9 %copy-start.9 = (s32[2]{0:T(128)S(1)}, s32[2]{0:T(128)}, u32[]{:S(2)}) copy-start(s32[2]{0:T(128)} %constant.190) | copy-start | bytes 28
  0.6 16.0 %copy-start.8 = (s32[2]{0:T(128)S(1)}, s32[2]{0:T(128)}, u32[]{:S(2)}) copy-start(s32[2]{0:T(128)} %constant.187) | copy-start | bytes 28
  0.7 16.1 %copy-start.6 = (f32[2,2,2048]{2,1,0:T(2,128)S(1)}, f32[2,2,2048]{2,1,0:T(2,128)}, u32[]{:S(2)}) copy-start(f32[2,2,2048]{2,1,0:T(2,128)} %param.21) | copy-start | bytes 98308
  0.7 16.1 %copy-start.7 = (s32[2]{0:T(128)S(1)}, s32[2]{0:T(128)}, u32[]{:S(2)}) copy-start(s32[2]{0:T(128)} %param.19) | copy-start | bytes 28
  0.7 16.2 %copy-start.5 = (f32[2,64,64]{2,1,0:T(8,128)S(1)}, f32[2,64,64]{2,1,0:T(8,128)}, u32[]{:S(2)}) copy-start(f32[2,64,64]{2,1,0:T(8,128)} %param.16) | copy-start | bytes 98308
  1.6 15.4 %collective-permute-start = (f32[1,64,128]{2,1,0:T(8,128)S(1)}, f32[1,64,128]{2,1,0:T(8,128)S(1)}, u32[]{:S(2)}, u32[]{:S(2)}) collective-permute-start(f32[1,64,128]{2,1,0:T(8,128)S(1)} %get-tuple-element.70), channel_id=1, source_target_pairs={{4,0},{8,4},{12,8},{5,1},{9,5},{13,9},{6,2},{10,6},{14,10},{7,3},{... | collective-permute-start | bytes 98312 | tf_op jit(solution)/shard_map/ppermute | solution.py:21
  2.9 14.1 %collective-permute-start.2 = (f32[1,64,128]{2,1,0:T(8,128)S(1)}, f32[1,64,128]{2,1,0:T(8,128)S(1)}, u32[]{:S(2)}, u32[]{:S(2)}) collective-permute-start(f32[1,64,128]{2,1,0:T(8,128)S(1)} %get-tuple-element.69), channel_id=1, source_target_pairs={{0,4},{4,8},{8,12},{1,5},{5,9},{9,13},{2,6},{6,10},{10,14},{3,7},{... | collective-permute-start | bytes 98312 | tf_op jit(solution)/shard_map/ppermute | solution.py:18
  9.4 24.3 %collective-permute-start.9 = (f32[2,1,64,128]{3,2,1,0:T(8,128)S(1)}, f32[2,1,64,128]{3,2,1,0:T(8,128)S(1)}, u32[]{:S(2)}, u32[]{:S(2)}) collective-permute-start(f32[2,1,64,128]{3,2,1,0:T(8,128)S(1)} %get-tuple-element.63), channel_id=1, source_target_pairs={{0,4},{4,8},{8,12},{1,5},{5,9},{9,13},{2,6},{6,10},{10,14},{3,7},{... | collective-permute-start | bytes 196616 | tf_op jit(solution)/shard_map/ppermute | solution.py:18
  13.3 20.4 %collective-permute-start.8 = (f32[2,1,64,128]{3,2,1,0:T(8,128)S(1)}, f32[2,1,64,128]{3,2,1,0:T(8,128)S(1)}, u32[]{:S(2)}, u32[]{:S(2)}) collective-permute-start(f32[2,1,64,128]{3,2,1,0:T(8,128)S(1)} %get-tuple-element.62), channel_id=1, source_target_pairs={{4,0},{8,4},{12,8},{5,1},{9,5},{13,9},{6,2},{10,6},{14,10},{7,3},{... | collective-permute-start | bytes 196616 | tf_op jit(solution)/shard_map/ppermute | solution.py:21
  16.8 9.8 %copy-start.2 = (f32[2,64,128]{2,1,0:T(8,128)S(1)}, f32[2,64,128]{2,1,0:T(8,128)}, u32[]{:S(2)}) copy-start(f32[2,64,128]{2,1,0:T(8,128)} %param.17) | copy-start | bytes 196612
  17.0 9.4 %collective-permute-start.4 = (f32[4,1,128]{2,1,0:T(1,128)S(1)}, f32[4,1,128]{2,1,0:T(1,128)S(1)}, u32[]{:S(2)}, u32[]{:S(2)}) collective-permute-start(f32[4,1,128]{2,1,0:T(1,128)S(1)} %get-tuple-element.61), channel_id=1, source_target_pairs={{1,0},{3,2},{5,4},{7,6},{9,8},{11,10},{13,12},{15,14},{17,16},{19,... | collective-permute-start | bytes 6152 | tf_op jit(solution)/shard_map/ppermute | solution.py:21
  18.3 8.1 %collective-permute-start.6 = (f32[4,1,128]{2,1,0:T(1,128)S(1)}, f32[4,1,128]{2,1,0:T(1,128)S(1)}, u32[]{:S(2)}, u32[]{:S(2)}) collective-permute-start(f32[4,1,128]{2,1,0:T(1,128)S(1)} %get-tuple-element.60), channel_id=1, source_target_pairs={{0,1},{2,3},{4,5},{6,7},{8,9},{10,11},{12,13},{14,15},{16,17},{18,... | collective-permute-start | bytes 6152 | tf_op jit(solution)/shard_map/ppermute | solution.py:18
  26.3 0.9 copy-start.1
  26.6 7.1 %copy-start = (f32[2,2,64,128]{3,2,1,0:T(8,128)S(1)}, f32[2,2,64,128]{3,2,1,0:T(8,128)}, u32[]{:S(2)}) copy-start(f32[2,2,64,128]{3,2,1,0:T(8,128)} %param.13) | copy-start | bytes 393220
  27.2 53.2 %collective-permute-start.1 = (f32[2,1,64,128]{3,2,1,0:T(8,128)S(1)}, f32[2,1,64,128]{3,2,1,0:T(8,128)S(1)}, u32[]{:S(2)}, u32[]{:S(2)}) collective-permute-start(f32[2,1,64,128]{3,2,1,0:T(8,128)S(1)} %get-tuple-element.55), channel_id=1, source_target_pairs={{4,0},{8,4},{12,8},{5,1},{9,5},{13,9},{6,2},{10,6},{14,10},{7,3},{... | collective-permute-start | bytes 196616 | tf_op jit(solution)/shard_map/ppermute | solution.py:21
  28.5 51.9 %collective-permute-start.3 = (f32[2,1,64,128]{3,2,1,0:T(8,128)S(1)}, f32[2,1,64,128]{3,2,1,0:T(8,128)S(1)}, u32[]{:S(2)}, u32[]{:S(2)}) collective-permute-start(f32[2,1,64,128]{3,2,1,0:T(8,128)S(1)} %get-tuple-element.54), channel_id=1, source_target_pairs={{0,4},{4,8},{8,12},{1,5},{5,9},{9,13},{2,6},{6,10},{10,14},{3,7},{... | collective-permute-start | bytes 196616 | tf_op jit(solution)/shard_map/ppermute | solution.py:18
  33.8 4.5 %collective-permute-start.10 = (f32[2,4,1,128]{3,2,1,0:T(1,128)S(1)}, f32[2,4,1,128]{3,2,1,0:T(1,128)S(1)}, u32[]{:S(2)}, u32[]{:S(2)}) collective-permute-start(f32[2,4,1,128]{3,2,1,0:T(1,128)S(1)} %get-tuple-element.45), channel_id=1, source_target_pairs={{1,0},{3,2},{5,4},{7,6},{9,8},{11,10},{13,12},{15,14},{17,16},{19,... | collective-permute-start | bytes 12296 | tf_op jit(solution)/shard_map/ppermute | solution.py:21
  35.1 4.2 %copy-start.4 = (f32[2,2,64,128]{3,2,1,0:T(8,128)S(1)}, f32[2,2,64,128]{3,2,1,0:T(8,128)}, u32[]{:S(2)}) copy-start(f32[2,2,64,128]{3,2,1,0:T(8,128)} %param.12) | copy-start | bytes 393220
  35.1 4.0 %collective-permute-start.11 = (f32[2,4,1,128]{3,2,1,0:T(1,128)S(1)}, f32[2,4,1,128]{3,2,1,0:T(1,128)S(1)}, u32[]{:S(2)}, u32[]{:S(2)}) collective-permute-start(f32[2,4,1,128]{3,2,1,0:T(1,128)S(1)} %get-tuple-element.44), channel_id=1, source_target_pairs={{0,1},{2,3},{4,5},{6,7},{8,9},{10,11},{12,13},{14,15},{16,17},{18,... | collective-permute-start | bytes 12296 | tf_op jit(solution)/shard_map/ppermute | solution.py:18
  40.3 45.6 %collective-permute-start.13 = (f32[2,1,64,128]{3,2,1,0:T(8,128)S(1)}, f32[2,1,64,128]{3,2,1,0:T(8,128)S(1)}, u32[]{:S(2)}, u32[]{:S(2)}) collective-permute-start(f32[2,1,64,128]{3,2,1,0:T(8,128)S(1)} %get-tuple-element.57), channel_id=1, source_target_pairs={{0,4},{4,8},{8,12},{1,5},{5,9},{9,13},{2,6},{6,10},{10,14},{3,7},{... | collective-permute-start | bytes 196616 | tf_op jit(solution)/shard_map/ppermute | solution.py:18
  44.2 41.7 %collective-permute-start.12 = (f32[2,1,64,128]{3,2,1,0:T(8,128)S(1)}, f32[2,1,64,128]{3,2,1,0:T(8,128)S(1)}, u32[]{:S(2)}, u32[]{:S(2)}) collective-permute-start(f32[2,1,64,128]{3,2,1,0:T(8,128)S(1)} %get-tuple-element.56), channel_id=1, source_target_pairs={{4,0},{8,4},{12,8},{5,1},{9,5},{13,9},{6,2},{10,6},{14,10},{7,3},{... | collective-permute-start | bytes 196616 | tf_op jit(solution)/shard_map/ppermute | solution.py:21
  80.4 4.4 %collective-permute-start.5 = (f32[2,4,1,128]{3,2,1,0:T(1,128)S(1)}, f32[2,4,1,128]{3,2,1,0:T(1,128)S(1)}, u32[]{:S(2)}, u32[]{:S(2)}) collective-permute-start(f32[2,4,1,128]{3,2,1,0:T(1,128)S(1)} %get-tuple-element.41), channel_id=1, source_target_pairs={{1,0},{3,2},{5,4},{7,6},{9,8},{11,10},{13,12},{15,14},{17,16},{19,... | collective-permute-start | bytes 12296 | tf_op jit(solution)/shard_map/ppermute | solution.py:21
  81.7 3.8 collective-permute-start.7
  84.8 5.4 %copy-start.3 = (f32[2,2,64,128]{3,2,1,0:T(8,128)S(1)}, f32[2,2,64,128]{3,2,1,0:T(8,128)}, u32[]{:S(2)}) copy-start(f32[2,2,64,128]{3,2,1,0:T(8,128)} %param.14) | copy-start | bytes 393220
  85.9 4.5 %collective-permute-start.14 = (f32[2,4,1,128]{3,2,1,0:T(1,128)S(1)}, f32[2,4,1,128]{3,2,1,0:T(1,128)S(1)}, u32[]{:S(2)}, u32[]{:S(2)}) collective-permute-start(f32[2,4,1,128]{3,2,1,0:T(1,128)S(1)} %get-tuple-element.43), channel_id=1, source_target_pairs={{1,0},{3,2},{5,4},{7,6},{9,8},{11,10},{13,12},{15,14},{17,16},{19,... | collective-permute-start | bytes 12296 | tf_op jit(solution)/shard_map/ppermute | solution.py:21
  87.2 3.8 collective-permute-start.15
  153.1 7.4 %collective-permute-start.16 = (f32[2,1,64,128]{3,2,1,0:T(8,128)S(1)}, f32[2,1,64,128]{3,2,1,0:T(8,128)S(1)}, u32[]{:S(2)}, u32[]{:S(2)}) collective-permute-start(f32[2,1,64,128]{3,2,1,0:T(8,128)S(1)} %get-tuple-element.53), channel_id=1, source_target_pairs={{4,0},{8,4},{12,8},{5,1},{9,5},{13,9},{6,2},{10,6},{14,10},{7,3},{... | collective-permute-start | bytes 196616 | tf_op jit(solution)/shard_map/ppermute | solution.py:21
  154.4 7.3 %collective-permute-start.17 = (f32[2,1,64,128]{3,2,1,0:T(8,128)S(1)}, f32[2,1,64,128]{3,2,1,0:T(8,128)S(1)}, u32[]{:S(2)}, u32[]{:S(2)}) collective-permute-start(f32[2,1,64,128]{3,2,1,0:T(8,128)S(1)} %get-tuple-element.52), channel_id=1, source_target_pairs={{0,4},{4,8},{8,12},{1,5},{5,9},{9,13},{2,6},{6,10},{10,14},{3,7},{... | collective-permute-start | bytes 196616 | tf_op jit(solution)/shard_map/ppermute | solution.py:18
  161.7 4.3 %collective-permute-start.18 = (f32[2,4,1,128]{3,2,1,0:T(1,128)S(1)}, f32[2,4,1,128]{3,2,1,0:T(1,128)S(1)}, u32[]{:S(2)}, u32[]{:S(2)}) collective-permute-start(f32[2,4,1,128]{3,2,1,0:T(1,128)S(1)} %get-tuple-element.39), channel_id=1, source_target_pairs={{1,0},{3,2},{5,4},{7,6},{9,8},{11,10},{13,12},{15,14},{17,16},{19,... | collective-permute-start | bytes 12296 | tf_op jit(solution)/shard_map/ppermute | solution.py:21
  163.0 3.8 collective-permute-start.19
  252.5 9.1 %collective-permute-start.25 = (f32[2,1,64,128]{3,2,1,0:T(8,128)S(1)}, f32[2,1,64,128]{3,2,1,0:T(8,128)S(1)}, u32[]{:S(2)}, u32[]{:S(2)}) collective-permute-start(f32[2,1,64,128]{3,2,1,0:T(8,128)S(1)} %get-tuple-element.51), channel_id=1, source_target_pairs={{0,4},{4,8},{8,12},{1,5},{5,9},{9,13},{2,6},{6,10},{10,14},{3,7},{... | collective-permute-start | bytes 196616 | tf_op jit(solution)/shard_map/ppermute | solution.py:18
  253.8 7.9 %collective-permute-start.24 = (f32[2,1,64,128]{3,2,1,0:T(8,128)S(1)}, f32[2,1,64,128]{3,2,1,0:T(8,128)S(1)}, u32[]{:S(2)}, u32[]{:S(2)}) collective-permute-start(f32[2,1,64,128]{3,2,1,0:T(8,128)S(1)} %get-tuple-element.50), channel_id=1, source_target_pairs={{4,0},{8,4},{12,8},{5,1},{9,5},{13,9},{6,2},{10,6},{14,10},{7,3},{... | collective-permute-start | bytes 196616 | tf_op jit(solution)/shard_map/ppermute | solution.py:21
  255.1 10.9 %collective-permute-start.20 = (f32[2,1,64,128]{3,2,1,0:T(8,128)S(1)}, f32[2,1,64,128]{3,2,1,0:T(8,128)S(1)}, u32[]{:S(2)}, u32[]{:S(2)}) collective-permute-start(f32[2,1,64,128]{3,2,1,0:T(8,128)S(1)} %get-tuple-element.49), channel_id=1, source_target_pairs={{4,0},{8,4},{12,8},{5,1},{9,5},{13,9},{6,2},{10,6},{14,10},{7,3},{... | collective-permute-start | bytes 196616 | tf_op jit(solution)/shard_map/ppermute | solution.py:21
  256.4 9.6 %collective-permute-start.21 = (f32[2,1,64,128]{3,2,1,0:T(8,128)S(1)}, f32[2,1,64,128]{3,2,1,0:T(8,128)S(1)}, u32[]{:S(2)}, u32[]{:S(2)}) collective-permute-start(f32[2,1,64,128]{3,2,1,0:T(8,128)S(1)} %get-tuple-element.48), channel_id=1, source_target_pairs={{0,4},{4,8},{8,12},{1,5},{5,9},{9,13},{2,6},{6,10},{10,14},{3,7},{... | collective-permute-start | bytes 196616 | tf_op jit(solution)/shard_map/ppermute | solution.py:18
  261.7 8.7 %collective-permute-start.26 = (f32[2,4,1,128]{3,2,1,0:T(1,128)S(1)}, f32[2,4,1,128]{3,2,1,0:T(1,128)S(1)}, u32[]{:S(2)}, u32[]{:S(2)}) collective-permute-start(f32[2,4,1,128]{3,2,1,0:T(1,128)S(1)} %get-tuple-element.37), channel_id=1, source_target_pairs={{1,0},{3,2},{5,4},{7,6},{9,8},{11,10},{13,12},{15,14},{17,16},{19,... | collective-permute-start | bytes 12296 | tf_op jit(solution)/shard_map/ppermute | solution.py:21
  263.0 7.4 %collective-permute-start.27 = (f32[2,4,1,128]{3,2,1,0:T(1,128)S(1)}, f32[2,4,1,128]{3,2,1,0:T(1,128)S(1)}, u32[]{:S(2)}, u32[]{:S(2)}) collective-permute-start(f32[2,4,1,128]{3,2,1,0:T(1,128)S(1)} %get-tuple-element.36), channel_id=1, source_target_pairs={{0,1},{2,3},{4,5},{6,7},{8,9},{10,11},{12,13},{14,15},{16,17},{18,... | collective-permute-start | bytes 12296 | tf_op jit(solution)/shard_map/ppermute | solution.py:18
  266.0 40.5 %collective-permute-start.22 = (f32[2,4,1,128]{3,2,1,0:T(1,128)S(1)}, f32[2,4,1,128]{3,2,1,0:T(1,128)S(1)}, u32[]{:S(2)}, u32[]{:S(2)}) collective-permute-start(f32[2,4,1,128]{3,2,1,0:T(1,128)S(1)} %get-tuple-element.35), channel_id=1, source_target_pairs={{1,0},{3,2},{5,4},{7,6},{9,8},{11,10},{13,12},{15,14},{17,16},{19,... | collective-permute-start | bytes 12296 | tf_op jit(solution)/shard_map/ppermute | solution.py:21
  267.3 39.2 %collective-permute-start.23 = (f32[2,4,1,128]{3,2,1,0:T(1,128)S(1)}, f32[2,4,1,128]{3,2,1,0:T(1,128)S(1)}, u32[]{:S(2)}, u32[]{:S(2)}) collective-permute-start(f32[2,4,1,128]{3,2,1,0:T(1,128)S(1)} %get-tuple-element.34), channel_id=1, source_target_pairs={{0,1},{2,3},{4,5},{6,7},{8,9},{10,11},{12,13},{14,15},{16,17},{18,... | collective-permute-start | bytes 12296 | tf_op jit(solution)/shard_map/ppermute | solution.py:18
  333.0 6.2 %collective-permute-start.28 = (f32[2,1,64,128]{3,2,1,0:T(8,128)S(1)}, f32[2,1,64,128]{3,2,1,0:T(8,128)S(1)}, u32[]{:S(2)}, u32[]{:S(2)}) collective-permute-start(f32[2,1,64,128]{3,2,1,0:T(8,128)S(1)} %get-tuple-element.47), channel_id=1, source_target_pairs={{4,0},{8,4},{12,8},{5,1},{9,5},{13,9},{6,2},{10,6},{14,10},{7,3},{... | collective-permute-start | bytes 196616 | tf_op jit(solution)/shard_map/ppermute | solution.py:21
  334.3 6.5 %collective-permute-start.29 = (f32[2,1,64,128]{3,2,1,0:T(8,128)S(1)}, f32[2,1,64,128]{3,2,1,0:T(8,128)S(1)}, u32[]{:S(2)}, u32[]{:S(2)}) collective-permute-start(f32[2,1,64,128]{3,2,1,0:T(8,128)S(1)} %get-tuple-element.46), channel_id=1, source_target_pairs={{0,4},{4,8},{8,12},{1,5},{5,9},{9,13},{2,6},{6,10},{10,14},{3,7},{... | collective-permute-start | bytes 196616 | tf_op jit(solution)/shard_map/ppermute | solution.py:18
  340.9 4.3 %collective-permute-start.30 = (f32[2,4,1,128]{3,2,1,0:T(1,128)S(1)}, f32[2,4,1,128]{3,2,1,0:T(1,128)S(1)}, u32[]{:S(2)}, u32[]{:S(2)}) collective-permute-start(f32[2,4,1,128]{3,2,1,0:T(1,128)S(1)} %get-tuple-element.33), channel_id=1, source_target_pairs={{1,0},{3,2},{5,4},{7,6},{9,8},{11,10},{13,12},{15,14},{17,16},{19,... | collective-permute-start | bytes 12296 | tf_op jit(solution)/shard_map/ppermute | solution.py:21
  342.1 3.8 collective-permute-start.31
